TPU v7x, 512 devices: a whole 4x4x16 slice. The times are simulated.
512 devices in a mesh: leaf: 32 (over x, y, core), blk: 16 (over z).
Axes of the slice: x: 4, y: 4, z: 16, core: 2. Of those that a mesh axis runs over, the one named last changes fastest.
Arguments:
- points: float32 [3, 131072], P(None, ('leaf', 'blk')), may hold values from 0 to 1
- iterate: bfloat16 [131072, 256], P(('leaf', 'blk')), may hold values from -6 to 6
- right_side: float32 [131072, 256], P(('leaf', 'blk')), may hold values from -6 to 6
- near_mask: int32 [512, 16], P(('leaf', 'blk')), may hold values from 0 to 1, as said below
- leaf_inverse: bfloat16 [512, 256, 256], P(('leaf', 'blk'))
- skeleton: int32 [3, 32, 512], P(None, 'leaf'), may hold values from 0 to 4095, as said below
- coupling: bfloat16 [3, 32, 512, 512], P(None, 'leaf'), may hold values from -0.25 to 0.25
- reduced_inverse: bfloat16 [3, 32, 512, 512], P(None, 'leaf')
- lift: bfloat16 [3, 131072, 512], P(None, ('leaf', 'blk')), may hold values from -0.25 to 0.25
Outputs:
- correction: float32 [131072, 256], P(('leaf', 'blk'))
Inputs may be any that keep to these rules, and one draw needn't show every extreme that they name: near_mask[i, i mod 16] is 1. `skeleton`: the 512 indices of one level and subtree are distinct.
All inputs are finite; a program needn't handle non-finite values.
Results may differ from a plain program's by a relative error of at most 0.014.
Values may be sent and summed in bfloat16 or wider, within the bound.
No kernel may reach another device: no remote copies, remote signals or barrier semaphores. Data moves between devices by JAX's collectives and lax.ppermute only.
A program may use at most 64 MiB of HBM per device.

v0:
```python
import jax
import jax.numpy as jnp
from jax import lax
from jax.sharding import PartitionSpec as P

LEVELS = 3
kernel_scale = 0.125
spread_coef = 4.0
shift_value = 1.0


def from_partner(block, axis, distance):
    count = lax.axis_size(axis)
    route = []
    for low in range(count):
        high = low | 1 << distance
        if high != low and high < count:
            route += [(low, high), (high, low)]
    return lax.ppermute(block, axis, route)


def kernel_block(left, right):
    dist = jnp.zeros((left.shape[1], right.shape[1]), jnp.float32)
    for axis_no in range(3):
        diff = left[axis_no][:, None] - right[axis_no][None, :]
        dist = dist + diff * diff
    return kernel_scale * jnp.exp(-spread_coef * dist)


def sibling_solve(cpl, inverse, part_total, level_no):
    own_total = part_total
    for bit_no in range(level_no):
        own_total = own_total + from_partner(own_total, "leaf", bit_no)
    other_total = from_partner(own_total.astype(jnp.bfloat16), "leaf", level_no).astype(
        own_total.dtype
    )
    rhs = own_total - jnp.dot(
        cpl, other_total.astype(jnp.bfloat16), preferred_element_type=jnp.float32
    )
    return jnp.dot(inverse, rhs.astype(jnp.bfloat16), preferred_element_type=jnp.float32)


def on_device(
    points, iterate, right_side, near_mask, leaf_inverse, skeleton, coupling, reduced_inverse, lift
):
    tile_rows = points.shape[1]
    all_pts = lax.all_gather(points, "blk", axis=1, tiled=True)
    mask_row = near_mask[0].astype(jnp.bfloat16)
    block_rows = lax.all_gather(iterate, "blk", axis=0, tiled=True)
    count = block_rows.shape[0]
    col_block = jnp.arange(count, dtype=jnp.int32) // tile_rows
    col_mask = jnp.take(mask_row, col_block)
    kernel = kernel_block(points, all_pts).astype(jnp.bfloat16)
    near = jnp.dot(kernel * col_mask[None, :], block_rows, preferred_element_type=jnp.float32)
    resid = right_side - shift_value * iterate.astype(jnp.float32) - near
    field = jnp.dot(leaf_inverse[0], resid.astype(jnp.bfloat16), preferred_element_type=jnp.float32)
    blk_start = lax.axis_index("blk") * tile_rows
    for level_no in range(LEVELS):
        local_index = skeleton[level_no, 0] - blk_start
        inside = (local_index >= 0) & (local_index < tile_rows)
        rows_taken = jnp.take(field, jnp.clip(local_index, 0, tile_rows - 1), axis=0)
        picked = jnp.where(inside[:, None], rows_taken, 0.0)
        part_total = lax.psum(picked, "blk")
        answer = sibling_solve(
            coupling[level_no, 0], reduced_inverse[level_no, 0], part_total, level_no
        ).astype(jnp.bfloat16)
        field = field - jnp.dot(lift[level_no], answer, preferred_element_type=jnp.float32)
    return field


def solution(mesh):
    in_specs = (
        P(None, ("leaf", "blk")),
        P(("leaf", "blk"), None),
        P(("leaf", "blk"), None),
        P(("leaf", "blk"), None),
        P(("leaf", "blk"), None, None),
        P(None, "leaf", None),
        P(None, "leaf", None, None),
        P(None, "leaf", None, None),
        P(None, ("leaf", "blk"), None),
    )
    out_specs = P(("leaf", "blk"), None)
    return jax.shard_map(
        on_device, mesh=mesh, in_specs=in_specs, out_specs=out_specs, check_vma=False
    )
```

profile of v0, /device:TPU:2, one launch (start us, length us, event | category | flops | bytes accessed | tf_op | source)
XLA Modules:
  0.0 568.9 jit_solution(15477949225896639626)
XLA Ops:
  6.5 0.0 copy-start
  6.5 0.0 all-gather.2.cloned.1.call-start
  6.5 0.7 all-gather.2.cloned.1.call-update
  7.3 0.0 all-reduce.4.cloned.1.call-start
  7.3 0.7 convert_element_type.53
  8.0 0.1 compare_reduce_fusion.1
  8.1 0.1 compare_reduce_fusion.2
  8.1 0.1 compare_reduce_fusion.3
  8.2 0.1 compare_reduce_fusion.4
  8.2 0.1 compare_reduce_fusion.5
  8.3 0.1 compare_reduce_fusion.6
  8.4 0.1 compare_reduce_fusion.7
  8.4 0.1 compare_reduce_fusion.8
  8.5 36.0 %all_gather.6 = f32[3,4096]{1,0:T(4,128)S(1)} all-gather(f32[3,256]{1,0:T(4,128)} %param.11), channel_id=1, replica_groups=mesh['leaf'=32,'blk'=16] {'blk'}, dimensions={1}, use_global_device_ids=true | all-gather | bytes 52224 | tf_op jit(solution)/shard_map/all_gather | solution.py:47
  44.5 0.7 fusion.79
  45.2 4.3 fusion.67
  49.5 0.7 broadcast_clamp_fusion
  50.2 0.8 and_reduce_fusion
  51.0 0.8 fusion.78
  51.8 5.7 %fusion.69 = bf16[4096]{0:T(1024)(128)(2,1)S(1)} fusion(pred[4096]{0:T(1024)(128)(4,1)S(1)} %compare_reduce_fusion, pred[4096]{0:T(1024)(128)(4,1)S(1)} %compare_reduce_fusion.1, pred[4096]{0:T(1024)(128)(4,1)S(1)} %compare_reduce_fusion.2, pred[4096]{0:T(1024)(128)(4,1)S(1)} %compare_reduce_fusion.3, pred[4096]{0:T(1024)(128)(4,1)S(1)} %compare_reduce_fusion.4, ...), kind=kLoop, calls=%fused_computation.94 | loop fusion | flops 98304 | bytes 53266 | tf_op jit(solution)/shard_map/jit(_take)/select_n | solution.py:52
  57.6 29.0 %all-gather.2.cloned.1.call-done = bf16[4096,256]{1,0:T(8,128)(2,1)} async-done(((bf16[256,256]{1,0:T(8,128)(2,1)}), bf16[4096,256]{1,0:T(8,128)(2,1)}) %all-gather.2.cloned.1.call-update) | async-done | bytes 2097168 | tf_op jit(solution)/shard_map/all_gather | solution.py:49
  86.6 0.0 copy-done
  86.6 3.9 convolution_bitcast_fusion.3
  90.5 0.1 copy.14
  90.7 1.6 gather_fusion
  92.3 0.0 copy-start.1
  92.3 1.0 select_select_fusion.2
  93.3 0.0 all-reduce.4.cloned.1.call-update
  93.3 0.0 all-reduce.6.cloned.1.call-start
  93.4 135.0 %all-reduce.4.cloned.1.call-done = f32[512,256]{1,0:T(8,128)} async-done(((f32[512,256]{1,0:T(8,128)}), f32[512,256]{1,0:T(8,128)}) %all-reduce.4.cloned.1.call-update) | async-done | bytes 524304 | tf_op jit(solution)/shard_map/psum | solution.py:63
  228.4 1.1 convert_element_type.56
  229.4 1.9 collective-permute-start
  231.4 1.5 collective-permute-done
  232.9 1.3 fusion.16
  234.2 1.6 fusion.25
  235.8 0.1 copy.15
  236.0 1.6 gather_fusion.1
  237.6 1.0 select_select_fusion.1
  238.6 0.0 all-reduce.6.cloned.1.call-update
  238.6 0.0 all-reduce.8.cloned.1.call-start
  238.7 134.5 %all-reduce.6.cloned.1.call-done = f32[512,256]{1,0:T(8,128)} async-done(((f32[512,256]{1,0:T(8,128)}), f32[512,256]{1,0:T(8,128)}) %all-reduce.6.cloned.1.call-update) | async-done | bytes 524304 | tf_op jit(solution)/shard_map/psum | solution.py:63
  373.2 1.9 collective-permute-start.1
  375.1 2.1 collective-permute-done.1
  377.2 1.1 fusion.76
  378.3 3.4 collective-permute-start.2
  381.7 6.8 %collective-permute-done.2 = bf16[512,256]{1,0:T(8,128)(2,1)S(1)} collective-permute-done((bf16[512,256]{1,0:T(8,128)(2,1)S(1)}, bf16[512,256]{1,0:T(8,128)(2,1)S(1)}, u32[]{:S(2)}, u32[]{:S(2)}) %collective-permute-start.2) | collective-permute-done | bytes 262176 | tf_op jit(solution)/shard_map/ppermute | solution.py:19
  388.5 0.3 fusion.15
  388.8 1.6 fusion.24
  390.4 0.1 copy.16
  390.5 1.6 gather_fusion.2
  392.1 1.0 select_select_fusion
  393.1 0.0 all-reduce.8.cloned.1.call-update
  393.2 134.6 %all-reduce.8.cloned.1.call-done = f32[512,256]{1,0:T(8,128)} async-done(((f32[512,256]{1,0:T(8,128)}), f32[512,256]{1,0:T(8,128)}) %all-reduce.8.cloned.1.call-update) | async-done | bytes 524304 | tf_op jit(solution)/shard_map/psum | solution.py:63
  527.8 1.9 collective-permute-start.3
  529.7 2.1 collective-permute-done.3
  531.8 1.1 add.73
  532.9 3.4 collective-permute-start.4
  536.3 12.5 %collective-permute-done.4 = f32[512,256]{1,0:T(8,128)S(1)} collective-permute-done((f32[512,256]{1,0:T(8,128)S(1)}, f32[512,256]{1,0:T(8,128)S(1)}, u32[]{:S(2)}, u32[]{:S(2)}) %collective-permute-start.4) | collective-permute-done | bytes 524320 | tf_op jit(solution)/shard_map/ppermute | solution.py:19
  548.7 0.1 fusion.75
  548.8 4.9 collective-permute-start.5
  553.7 6.0 %collective-permute-done.5 = bf16[512,256]{1,0:T(8,128)(2,1)S(1)} collective-permute-done((bf16[512,256]{1,0:T(8,128)(2,1)S(1)}, bf16[512,256]{1,0:T(8,128)(2,1)S(1)}, u32[]{:S(2)}, u32[]{:S(2)}) %collective-permute-start.5) | collective-permute-done | bytes 262176 | tf_op jit(solution)/shard_map/ppermute | solution.py:19
  559.7 0.3 fusion.14
  560.0 1.6 fusion.23
  561.6 0.8 copy.17
  (14 shorter events, 0.1 us)
Async XLA Ops:
  6.5 80.1 %copy-start = (bf16[1,256,256]{2,1,0:T(8,128)(2,1)S(1)}, bf16[1,256,256]{2,1,0:T(8,128)(2,1)}, u32[]{:S(2)}) copy-start(bf16[1,256,256]{2,1,0:T(8,128)(2,1)} %param.15) | copy-start | bytes 393220
  6.5 80.1 %all-gather.2.cloned.1.call-start = ((), (), s32[]{:S(2)}) async-start(), calls=%async_computation | async-start | bytes 2228224 | tf_op jit(solution)/shard_map/all_gather | solution.py:49
  7.3 221.1 %all-reduce.4.cloned.1.call-start = ((), (), s32[]{:S(2)}) async-start(), calls=%async_computation.1 | async-start | bytes 1048576 | tf_op jit(solution)/shard_map/psum | solution.py:63
  92.3 140.6 %copy-start.1 = (bf16[3,1,512,512]{3,2,1,0:T(8,128)(2,1)S(1)}, bf16[3,1,512,512]{3,2,1,0:T(8,128)(2,1)}, u32[]{:S(2)}) copy-start(bf16[3,1,512,512]{3,2,1,0:T(8,128)(2,1)} %param.17) | copy-start | bytes 4718596
  93.3 279.9 %all-reduce.6.cloned.1.call-start = ((), (), s32[]{:S(2)}) async-start(), calls=%async_computation.2 | async-start | bytes 1048576 | tf_op jit(solution)/shard_map/psum | solution.py:63
  229.4 3.4 collective-permute-start
  238.6 150.2 %copy-start.2 = (bf16[3,256,512]{2,1,0:T(8,128)(2,1)S(1)}, bf16[3,256,512]{2,1,0:T(8,128)(2,1)}, u32[]{:S(2)}) copy-start(bf16[3,256,512]{2,1,0:T(8,128)(2,1)} %param.19) | copy-start | bytes 2359300
  238.6 289.2 %all-reduce.8.cloned.1.call-start = ((), (), s32[]{:S(2)}) async-start(), calls=%async_computation.3 | async-start | bytes 1048576 | tf_op jit(solution)/shard_map/psum | solution.py:63
  373.2 4.0 collective-permute-start.1
  378.3 10.2 %collective-permute-start.2 = (bf16[512,256]{1,0:T(8,128)(2,1)S(1)}, bf16[512,256]{1,0:T(8,128)(2,1)S(1)}, u32[]{:S(2)}, u32[]{:S(2)}) collective-permute-start(bf16[512,256]{1,0:T(8,128)(2,1)S(1)} %get-tuple-element.11), channel_id=1, source_target_pairs={{0,32},{32,0},{16,48},{48,16},{64,96},{96,64},{80,112},{112,80},{1... | collective-permute-start | bytes 786440 | tf_op jit(solution)/shard_map/ppermute | solution.py:19
  527.8 4.0 collective-permute-start.3
  532.9 15.9 %collective-permute-start.4 = (f32[512,256]{1,0:T(8,128)S(1)}, f32[512,256]{1,0:T(8,128)S(1)}, u32[]{:S(2)}, u32[]{:S(2)}) collective-permute-start(f32[512,256]{1,0:T(8,128)S(1)} %add.73), channel_id=1, source_target_pairs={{0,32},{32,0},{16,48},{48,16},{64,96},{96,64},{80,112},{112,80},{1... | collective-permute-start | bytes 1572872 | tf_op jit(solution)/shard_map/ppermute | solution.py:19
  548.8 10.9 %collective-permute-start.5 = (bf16[512,256]{1,0:T(8,128)(2,1)S(1)}, bf16[512,256]{1,0:T(8,128)(2,1)S(1)}, u32[]{:S(2)}, u32[]{:S(2)}) collective-permute-start(bf16[512,256]{1,0:T(8,128)(2,1)S(1)} %get-tuple-element.9), channel_id=1, source_target_pairs={{0,64},{64,0},{16,80},{80,16},{32,96},{96,32},{48,112},{112,48},{1... | collective-permute-start | bytes 786440 | tf_op jit(solution)/shard_map/ppermute | solution.py:19
Sparse Core Ops, SparseCore 0:
  9.4 77.1 all-gather.1
  93.4 134.8 all-reduce.3
  238.7 134.3 all-reduce.5
  393.3 134.4 all-reduce.7
where the time goes:
time: 570 us; the launch traced here: 569 us
  waiting for transfers between devices  465 us (82%)
  blocking collectives  36 us (6%)
  other arithmetic  19.1 us (3%)
  starting transfers between devices  17.6 us (3%)
  between operations  13.4 us (2%)
  matrix products  10.6 us (2%)
  local copies, waits for them, and re-layouts  7.5 us (1%)
    psum x3, waiting for transfers between devices, on_device(): part_total = lax.psum(picked, 'blk')  404 us
    all_gather x1, blocking collectives, on_device(): all_pts = lax.all_gather(points, 'blk', axis=1, tiled=True)  36 us
    ppermute x6, waiting for transfers between devices, from_partner(): return lax.ppermute(block, axis, route)  30.9 us
    all_gather x1, waiting for transfers between devices, on_device(): block_rows = lax.all_gather(iterate, 'blk', axis=0, tiled=True)  29 us
    ppermute x6, starting transfers between devices, from_partner(): return lax.ppermute(block, axis, route)  17.4 us
  transfers between devices with their start and end apart: 10, of which 10 were waited for; matrix products, arithmetic and copies ran while one was open for 3% of the time, Pallas kernels for 0%

commit v1 on v0

--- a/solution.py
+++ b/solution.py
@@ -46,7 +46,10 @@
     tile_rows = points.shape[1]
     all_pts = lax.all_gather(points, "blk", axis=1, tiled=True)
     mask_row = near_mask[0].astype(jnp.bfloat16)
-    block_rows = lax.all_gather(iterate, "blk", axis=0, tiled=True)
+    size = lax.axis_size("blk")
+    shards = jnp.stack([iterate for _ in range(size)])
+    shards = lax.all_to_all(shards, "blk", split_axis=0, concat_axis=0)
+    block_rows = jnp.concatenate(shards, axis=0)
     count = block_rows.shape[0]
     col_block = jnp.arange(count, dtype=jnp.int32) // tile_rows
     col_mask = jnp.take(mask_row, col_block)

time: 570 us -> 635 us (1.11)
  blocking collectives: 36 us -> 116 us
  waiting for transfers between devices: 465 us -> 437 us
  starting transfers between devices: 17.6 us -> 32.9 us
    all_gather x1, blocking collectives: 36 us -> 116 us  [on_device(): all_pts = lax.all_gather(points, 'blk', axis=1, tiled=True)]
    all_gather x1 -> x0, waiting for transfers between devices: 29 us -> none  [on_device(): block_rows = lax.all_gather(iterate, 'blk', axis=0, tiled=True)]
    all_to_all x0 -> x1, starting transfers between devices: none -> 15.3 us  [on_device(): shards = lax.all_to_all(shards, 'blk', split_axis=0, concat_axis=0)]
  transfers between devices with their start and end apart: 10 -> 10, of which waited for: 10 -> 9; matrix products, arithmetic and copies ran while one was open for 3% -> 2% of each run, Pallas kernels for 0% -> 0%
where the time goes in v1:
time: 635 us; the launch traced here: 634 us
  waiting for transfers between devices  437 us (69%)
  blocking collectives  116 us (18%)
  starting transfers between devices  32.9 us (5%)
  other arithmetic  17.1 us (3%)
  between operations  13.5 us (2%)
  local copies, waits for them, and re-layouts  9.21 us (1%)
  matrix products  9.06 us (1%)
    psum x3, waiting for transfers between devices, on_device(): part_total = lax.psum(picked, 'blk')  406 us
    all_gather x1, blocking collectives, on_device(): all_pts = lax.all_gather(points, 'blk', axis=1, tiled=True)  116 us
    ppermute x6, waiting for transfers between devices, from_partner(): return lax.ppermute(block, axis, route)  30.9 us
    ppermute x6, starting transfers between devices, from_partner(): return lax.ppermute(block, axis, route)  17.4 us
    all_to_all x1, starting transfers between devices, on_device(): shards = lax.all_to_all(shards, 'blk', split_axis=0, concat_axis=0)  15.3 us
  transfers between devices with their start and end apart: 10, of which 9 were waited for; matrix products, arithmetic and copies ran while one was open for 2% of the time, Pallas kernels for 0%

profile of v1, /device:TPU:2, one launch (start us, length us, event | category | flops | bytes accessed | tf_op | source)
XLA Modules:
  0.0 634.5 jit_solution(17288810654655032047)
XLA Ops:
  6.5 0.0 copy-start
  6.5 2.5 stack.2
  9.0 0.0 copy-start.5
  9.1 15.3 %all-to-all-start = ((bf16[16,256,256]{2,1,0:T(8,128)(2,1)}), bf16[16,256,256]{2,1,0:T(8,128)(2,1)S(1)}, u32[]{:S(2)}, u32[]{:S(2)}) async-start(bf16[16,256,256]{2,1,0:T(8,128)(2,1)} %stack.2), calls=%async_computation | async-start | bytes 4194304 | tf_op jit(solution)/shard_map/all_to_all | solution.py:51
  24.4 0.0 all-reduce.4.cloned.1.call-start
  24.5 0.0 copy-done.6
  24.5 0.1 compare_reduce_fusion
  24.5 0.1 compare_reduce_fusion.1
  24.6 0.1 compare_reduce_fusion.2
  24.7 0.1 compare_reduce_fusion.3
  24.7 0.1 compare_reduce_fusion.4
  24.8 0.1 compare_reduce_fusion.5
  24.8 0.1 compare_reduce_fusion.6
  24.9 0.1 compare_reduce_fusion.7
  25.0 0.1 compare_reduce_fusion.8
  25.0 0.0 copy-done.4
  25.0 115.7 %all_gather.3 = f32[3,4096]{1,0:T(4,128)S(1)} all-gather(f32[3,256]{1,0:T(4,128)S(1)} %copy-done.4), channel_id=1, replica_groups=mesh['leaf'=32,'blk'=16] {'blk'}, dimensions={1}, use_global_device_ids=true | all-gather | bytes 52224 | tf_op jit(solution)/shard_map/all_gather | solution.py:47
  140.8 0.7 fusion.79
  141.5 4.3 fusion.67
  145.8 0.0 copy-done.3
  145.9 5.7 fusion.69
  151.7 0.0 all-to-all-done
  151.7 2.2 convolution_bitcast_fusion.3
  154.0 0.1 copy.14
  154.1 1.6 gather_fusion
  155.7 0.0 copy-start.1
  155.7 1.0 select_select_fusion.2
  156.7 0.0 all-reduce.4.cloned.1.call-update
  156.7 0.0 all-reduce.6.cloned.1.call-start
  156.8 137.0 %all-reduce.4.cloned.1.call-done = f32[512,256]{1,0:T(8,128)} async-done(((f32[512,256]{1,0:T(8,128)}), f32[512,256]{1,0:T(8,128)}) %all-reduce.4.cloned.1.call-update) | async-done | bytes 524304 | tf_op jit(solution)/shard_map/psum | solution.py:66
  293.8 1.1 convert_element_type.56
  294.8 1.9 collective-permute-start
  296.8 1.5 collective-permute-done
  298.3 1.3 fusion.16
  299.6 1.6 fusion.25
  301.3 0.1 copy.15
  301.4 1.6 gather_fusion.1
  303.0 1.0 select_select_fusion.1
  304.0 0.0 all-reduce.6.cloned.1.call-update
  304.0 0.0 all-reduce.8.cloned.1.call-start
  304.1 134.5 %all-reduce.6.cloned.1.call-done = f32[512,256]{1,0:T(8,128)} async-done(((f32[512,256]{1,0:T(8,128)}), f32[512,256]{1,0:T(8,128)}) %all-reduce.6.cloned.1.call-update) | async-done | bytes 524304 | tf_op jit(solution)/shard_map/psum | solution.py:66
  438.6 1.9 collective-permute-start.1
  440.5 2.1 collective-permute-done.1
  442.6 1.2 fusion.76
  443.7 3.4 collective-permute-start.2
  447.2 6.8 %collective-permute-done.2 = bf16[512,256]{1,0:T(8,128)(2,1)S(1)} collective-permute-done((bf16[512,256]{1,0:T(8,128)(2,1)S(1)}, bf16[512,256]{1,0:T(8,128)(2,1)S(1)}, u32[]{:S(2)}, u32[]{:S(2)}) %collective-permute-start.2) | collective-permute-done | bytes 262176 | tf_op jit(solution)/shard_map/ppermute | solution.py:19
  454.0 0.3 fusion.15
  454.3 1.6 fusion.24
  455.9 0.1 copy.16
  456.1 1.6 gather_fusion.2
  457.6 1.0 select_select_fusion
  458.7 0.0 all-reduce.8.cloned.1.call-update
  458.7 134.5 %all-reduce.8.cloned.1.call-done = f32[512,256]{1,0:T(8,128)} async-done(((f32[512,256]{1,0:T(8,128)}), f32[512,256]{1,0:T(8,128)}) %all-reduce.8.cloned.1.call-update) | async-done | bytes 524304 | tf_op jit(solution)/shard_map/psum | solution.py:66
  593.2 1.9 collective-permute-start.3
  595.1 2.1 collective-permute-done.3
  597.2 1.1 add.73
  598.3 3.4 collective-permute-start.4
  601.7 12.5 %collective-permute-done.4 = f32[512,256]{1,0:T(8,128)S(1)} collective-permute-done((f32[512,256]{1,0:T(8,128)S(1)}, f32[512,256]{1,0:T(8,128)S(1)}, u32[]{:S(2)}, u32[]{:S(2)}) %collective-permute-start.4) | collective-permute-done | bytes 524320 | tf_op jit(solution)/shard_map/ppermute | solution.py:19
  614.2 0.1 fusion.75
  614.3 4.9 collective-permute-start.5
  619.2 6.0 collective-permute-done.5
  625.1 0.3 fusion.14
  625.5 1.6 fusion.23
  627.1 0.8 copy.17
  (22 shorter events, 0.2 us)
Async XLA Ops:
  6.5 145.1 %copy-start = (bf16[1,256,256]{2,1,0:T(8,128)(2,1)S(1)}, bf16[1,256,256]{2,1,0:T(8,128)(2,1)}, u32[]{:S(2)}) copy-start(bf16[1,256,256]{2,1,0:T(8,128)(2,1)} %param.15) | copy-start | bytes 393220
  9.0 15.4 %copy-start.6 = (s32[1,16]{1,0:T(1,128)S(1)}, s32[1,16]{1,0:T(1,128)}, u32[]{:S(2)}) copy-start(s32[1,16]{1,0:T(1,128)} %param.14) | copy-start | bytes 196
  9.0 16.0 %copy-start.4 = (f32[3,256]{1,0:T(4,128)S(1)}, f32[3,256]{1,0:T(4,128)}, u32[]{:S(2)}) copy-start(f32[3,256]{1,0:T(4,128)} %param.11) | copy-start | bytes 9220
  9.0 136.7 %copy-start.3 = (s32[3,1,512]{2,1,0:T(1,128)S(1)}, s32[3,1,512]{2,1,0:T(1,128)}, u32[]{:S(2)}) copy-start(s32[3,1,512]{2,1,0:T(1,128)} %param.16) | copy-start | bytes 18436
  9.0 142.7 %copy-start.2 = (bf16[256,256]{1,0:T(8,128)(2,1)S(1)}, bf16[256,256]{1,0:T(8,128)(2,1)}, u32[]{:S(2)}) copy-start(bf16[256,256]{1,0:T(8,128)(2,1)} %param.12) | copy-start | bytes 393220
  9.0 142.7 %copy-start.5 = (f32[256,256]{1,0:T(8,128)S(1)}, f32[256,256]{1,0:T(8,128)}, u32[]{:S(2)}) copy-start(f32[256,256]{1,0:T(8,128)} %param.13) | copy-start | bytes 786436
  9.1 142.6 %all-to-all-start = ((bf16[16,256,256]{2,1,0:T(8,128)(2,1)}), bf16[16,256,256]{2,1,0:T(8,128)(2,1)S(1)}, u32[]{:S(2)}, u32[]{:S(2)}) async-start(bf16[16,256,256]{2,1,0:T(8,128)(2,1)} %stack.2), calls=%async_computation | async-start | bytes 4194304 | tf_op jit(solution)/shard_map/all_to_all | solution.py:51
  24.4 269.4 %all-reduce.4.cloned.1.call-start = ((), (), s32[]{:S(2)}) async-start(), calls=%async_computation.1 | async-start | bytes 1048576 | tf_op jit(solution)/shard_map/psum | solution.py:66
  155.7 142.6 %copy-start.1 = (bf16[3,1,512,512]{3,2,1,0:T(8,128)(2,1)S(1)}, bf16[3,1,512,512]{3,2,1,0:T(8,128)(2,1)}, u32[]{:S(2)}) copy-start(bf16[3,1,512,512]{3,2,1,0:T(8,128)(2,1)} %param.17) | copy-start | bytes 4718596
  156.7 281.8 %all-reduce.6.cloned.1.call-start = ((), (), s32[]{:S(2)}) async-start(), calls=%async_computation.2 | async-start | bytes 1048576 | tf_op jit(solution)/shard_map/psum | solution.py:66
  294.8 3.4 collective-permute-start
  304.0 289.2 %all-reduce.8.cloned.1.call-start = ((), (), s32[]{:S(2)}) async-start(), calls=%async_computation.3 | async-start | bytes 1048576 | tf_op jit(solution)/shard_map/psum | solution.py:66
  438.6 4.0 collective-permute-start.1
  443.7 10.2 %collective-permute-start.2 = (bf16[512,256]{1,0:T(8,128)(2,1)S(1)}, bf16[512,256]{1,0:T(8,128)(2,1)S(1)}, u32[]{:S(2)}, u32[]{:S(2)}) collective-permute-start(bf16[512,256]{1,0:T(8,128)(2,1)S(1)} %get-tuple-element.11), channel_id=1, source_target_pairs={{0,32},{32,0},{16,48},{48,16},{64,96},{96,64},{80,112},{112,80},{1... | collective-permute-start | bytes 786440 | tf_op jit(solution)/shard_map/ppermute | solution.py:19
  593.2 4.0 collective-permute-start.3
  598.3 15.9 %collective-permute-start.4 = (f32[512,256]{1,0:T(8,128)S(1)}, f32[512,256]{1,0:T(8,128)S(1)}, u32[]{:S(2)}, u32[]{:S(2)}) collective-permute-start(f32[512,256]{1,0:T(8,128)S(1)} %add.73), channel_id=1, source_target_pairs={{0,32},{32,0},{16,48},{48,16},{64,96},{96,64},{80,112},{112,80},{1... | collective-permute-start | bytes 1572872 | tf_op jit(solution)/shard_map/ppermute | solution.py:19
  614.3 10.9 %collective-permute-start.5 = (bf16[512,256]{1,0:T(8,128)(2,1)S(1)}, bf16[512,256]{1,0:T(8,128)(2,1)S(1)}, u32[]{:S(2)}, u32[]{:S(2)}) collective-permute-start(bf16[512,256]{1,0:T(8,128)(2,1)S(1)} %get-tuple-element.9), channel_id=1, source_target_pairs={{0,64},{64,0},{16,80},{80,16},{32,96},{96,32},{48,112},{112,48},{1... | collective-permute-start | bytes 786440 | tf_op jit(solution)/shard_map/ppermute | solution.py:19
Sparse Core Ops, SparseCore 0:
  156.9 136.8 all-reduce.3
  304.1 134.4 all-reduce.5
  458.8 134.3 all-reduce.7
